TPU v7x, 128 devices: a whole 4x4x4 slice. The times are simulated.
128 devices in a mesh: dp: 32 (over z, x, core), head: 4 (over y).
Axes of the slice: x: 4, y: 4, z: 4, core: 2. Of those that a mesh axis runs over, the one named last changes fastest.
Arguments:
- hidden: bfloat16 [1024, 2048], P('dp'), may hold values from -6 to 6
- attn_gain: float32 [2048], replicated, may hold values from 0.1 to 1.9
- w_query: bfloat16 [2048, 3072], P(None, 'head'), may hold values from -0.125 to 0.125
- w_latent: bfloat16 [2048, 576], P(None, 'head'), may hold values from -0.125 to 0.125
- latent_gain: float32 [512], replicated, may hold values from 0.1 to 1.9
- w_key_up: bfloat16 [16, 128, 512], P('head'), may hold values from -0.5 to 0.5
- w_value_up: bfloat16 [16, 512, 128], P('head'), may hold values from -0.25 to 0.25
- w_out: bfloat16 [2048, 2048], P('head'), may hold values from -0.125 to 0.125
- kv_cache: bfloat16 [1024, 128, 576], P('dp'), may hold values from -110 to 110
- lengths: int32 [1024], P('dp'), may hold values from 1 to 128, 65536 in all
- live_mask: int32 [1024], P('dp'), may hold values 0 or 1
- mlp_gain: float32 [2048], replicated, may hold values from 0.1 to 1.9
- w_router: bfloat16 [2048, 64], replicated, may hold values from -0.125 to 0.125
- routes: int32 [1024, 6], P('dp'), may hold values from 0 to 63, all different within a row; in each aligned block of 32 rows (0 to 31, 32 to 63, ...) at most 6 rows name the same one
- w_experts_in: bfloat16 [64, 2048, 2, 1408], P('dp', None, None, 'head'), may hold values from -0.125 to 0.125
- w_experts_out: bfloat16 [64, 1408, 2048], P('dp', 'head'), may hold values from -0.15625 to 0.15625
- w_shared_in: bfloat16 [2048, 2, 1408], P(None, None, 'head'), may hold values from -0.125 to 0.125
- w_shared_out: bfloat16 [1408, 2048], P('head'), may hold values from -0.15625 to 0.15625
Outputs:
- output: bfloat16 [1024, 2048], P('dp', 'head')
Inputs may be any that keep to these rules, and one draw needn't show every extreme that they name: Among the routes of one device's 32 rows no expert is named more than 6 times, a bound that some block reaches. Request t has cached positions 0 to lengths[t] - 1; some request has 128.
All inputs are finite; a program needn't handle non-finite values. No bound on the sum of `lengths` or of `live_mask` on one device may be relied on, other than what follows from the above.
Results may differ from a plain program's by a relative error of at most 0.02.
The roundings to bfloat16 on the way count: a program that leaves them out, or rounds other values in their place, can miss the bound.
Values may be sent and summed in bfloat16 or wider, within the bound.
A program may use at most 128 MiB of HBM per device.

v0:
```python
import math
import jax
import jax.numpy as jnp
from jax import lax
from jax.sharding import PartitionSpec as P

NOPE = 128
ROPE = 64
VDIM = 128
LAT = 512
norm_eps = 1e-06
rope_theta = 50000.0
route_scale = 2.446


def rms_norm(values, weights):
    mean_square = jnp.mean(values * values, axis=-1, keepdims=True)
    return values * lax.rsqrt(mean_square + norm_eps) * weights


def rotary(values, positions):
    half_size = values.shape[-1] // 2
    frequency = rope_theta ** (-jnp.arange(half_size, dtype=jnp.float32) / half_size)
    angles = positions.reshape((-1,) + (1,) * (values.ndim - 1)) * frequency
    first_half = values[..., :half_size]
    second_half = values[..., half_size:]
    cosine = jnp.cos(angles)
    sine_part = jnp.sin(angles)
    return jnp.concatenate(
        [
            first_half * cosine - second_half * sine_part,
            second_half * cosine + first_half * sine_part,
        ],
        axis=-1,
    )


def body(
    hidden,
    attn_gain,
    w_query,
    w_latent,
    latent_gain,
    w_key_up,
    w_value_up,
    w_out,
    kv_cache,
    lengths,
    live_mask,
    mlp_gain,
    w_router,
    routes,
    w_experts_in,
    w_experts_out,
    w_shared_in,
    w_shared_out,
):
    request_count = hidden.shape[0]
    model_width = hidden.shape[1]
    local_heads = w_key_up.shape[0]
    cache_length = kv_cache.shape[1]
    head_count = lax.axis_size("head")
    share_width = model_width // head_count
    column_start = lax.axis_index("head") * share_width
    dp_count = lax.axis_size("dp")
    local_experts = w_experts_in.shape[0]
    expert_total = local_experts * dp_count
    top_count = routes.shape[1]
    capacity = max(2, 2 * top_count * request_count // expert_total)
    normed = rms_norm(hidden.astype(jnp.float32), attn_gain).astype(jnp.bfloat16)
    query_all = jnp.dot(normed, w_query, preferred_element_type=jnp.float32).reshape(
        request_count, local_heads, NOPE + ROPE
    )
    positions = lengths.astype(jnp.float32)
    query_nope = query_all[..., :NOPE].astype(jnp.bfloat16)
    query_rope = rotary(query_all[..., NOPE:], positions).astype(jnp.bfloat16)
    query_latent = jnp.einsum(
        "rhn,hnc->rhc", query_nope, w_key_up, preferred_element_type=jnp.float32
    ).astype(jnp.bfloat16)
    fresh_part = jnp.dot(normed, w_latent, preferred_element_type=jnp.float32).astype(jnp.bfloat16)
    fresh_kv = lax.all_gather(fresh_part, "head", axis=1, tiled=True)
    latent_new = rms_norm(fresh_kv[:, :LAT].astype(jnp.float32), latent_gain)
    rope_new = rotary(fresh_kv[:, LAT:].astype(jnp.float32), positions)
    key_new = jnp.concatenate([latent_new, rope_new], axis=-1).astype(jnp.bfloat16)
    query_full = jnp.concatenate([query_latent, query_rope], axis=-1)
    inverse_root = 1.0 / math.sqrt(NOPE + ROPE)
    scores = (
        jnp.einsum("rhc,rjc->rhj", query_full, kv_cache, preferred_element_type=jnp.float32)
        * inverse_root
    )
    in_cache = jnp.arange(cache_length, dtype=jnp.int32)[None, :] < lengths[:, None]
    scores = jnp.where(in_cache[:, None, :], scores, -jnp.inf)
    score_new = (
        jnp.einsum("rhc,rc->rh", query_full, key_new, preferred_element_type=jnp.float32)
        * inverse_root
    )
    highest = jnp.maximum(jnp.max(scores, axis=-1), score_new)
    weights_cached = jnp.exp(scores - highest[..., None])
    weight_new = jnp.exp(score_new - highest)
    denominator = jnp.sum(weights_cached, axis=-1) + weight_new
    probabilities = (weights_cached / denominator[..., None]).astype(jnp.bfloat16)
    prob_new = (weight_new / denominator).astype(jnp.bfloat16)
    context = jnp.einsum(
        "rhj,rjc->rhc", probabilities, kv_cache[..., :LAT], preferred_element_type=jnp.float32
    )
    context = (
        context
        + prob_new.astype(jnp.float32)[..., None] * key_new[:, None, :LAT].astype(jnp.float32)
    ).astype(jnp.bfloat16)
    values = jnp.einsum(
        "rhc,hcv->rhv", context, w_value_up, preferred_element_type=jnp.float32
    ).astype(jnp.bfloat16)
    partial_value = jnp.dot(
        values.reshape(request_count, local_heads * VDIM), w_out, preferred_element_type=jnp.float32
    )
    attention = lax.psum(partial_value.astype(jnp.bfloat16), "head").astype(jnp.float32)
    mixed_rows = (hidden.astype(jnp.float32) + attention).astype(jnp.bfloat16)
    ffn_input = rms_norm(mixed_rows.astype(jnp.float32), mlp_gain).astype(jnp.bfloat16)
    mixed_share = lax.dynamic_slice_in_dim(mixed_rows, column_start, share_width, 1)
    logits = jnp.dot(ffn_input, w_router, preferred_element_type=jnp.float32)
    chosen = jax.nn.sigmoid(jnp.take_along_axis(logits, routes, axis=1))
    route_weight = (
        route_scale
        * live_mask.astype(jnp.float32)[:, None]
        * chosen
        / jnp.sum(chosen, axis=1, keepdims=True)
    )
    pair_count = request_count * top_count
    flat_routes = routes.reshape(pair_count)
    live_pairs = jnp.repeat(live_mask, top_count)
    member = (
        (flat_routes[:, None] == jnp.arange(expert_total, dtype=jnp.int32)[None, :])
        & (live_pairs[:, None] == 1)
    ).astype(jnp.int32)
    earlier = jnp.cumsum(member, axis=0) - member
    slot_rank = jnp.sum(earlier * member, axis=1)
    slot_total = expert_total * capacity
    buffer_slot = jnp.where(live_pairs == 1, flat_routes * capacity + slot_rank, slot_total)
    token_of_pair = jnp.arange(pair_count, dtype=jnp.int32) // top_count
    spread = ffn_input[token_of_pair]
    packed = (
        jnp.zeros((slot_total, ffn_input.shape[1]), jnp.bfloat16)
        .at[buffer_slot]
        .set(spread, mode="drop")
    )
    arrived = lax.all_to_all(
        packed.reshape(dp_count, local_experts, capacity, ffn_input.shape[1]),
        "dp",
        split_axis=0,
        concat_axis=0,
        tiled=True,
    )
    gate_up = jnp.einsum(
        "secd,edkf->seckf", arrived, w_experts_in, preferred_element_type=jnp.float32
    )
    acting = (jax.nn.silu(gate_up[..., 0, :]) * gate_up[..., 1, :]).astype(jnp.bfloat16)
    expert_part = jnp.einsum(
        "secf,efd->secd", acting, w_experts_out, preferred_element_type=jnp.float32
    )
    expert_share = lax.psum_scatter(
        expert_part.astype(jnp.bfloat16), "head", scatter_dimension=3, tiled=True
    )
    returned = lax.all_to_all(expert_share, "dp", split_axis=0, concat_axis=0, tiled=True)
    returned_rows = returned.reshape(slot_total, share_width)
    pick_slot = jnp.minimum(buffer_slot, slot_total - 1)
    pair_rows = returned_rows[pick_slot].astype(jnp.float32)
    routed = jnp.sum(
        (route_weight.reshape(pair_count)[:, None] * pair_rows).reshape(
            request_count, top_count, share_width
        ),
        axis=1,
    )
    shared_width = w_shared_out.shape[0]
    shared_pair = jnp.dot(
        ffn_input,
        w_shared_in.reshape(model_width, 2 * shared_width),
        preferred_element_type=jnp.float32,
    ).reshape(request_count, 2, shared_width)
    shared_act = (jax.nn.silu(shared_pair[:, 0]) * shared_pair[:, 1]).astype(jnp.bfloat16)
    shared_part = jnp.dot(shared_act, w_shared_out, preferred_element_type=jnp.float32)
    shared_share = lax.psum_scatter(
        shared_part.astype(jnp.bfloat16), "head", scatter_dimension=1, tiled=True
    ).astype(jnp.float32)
    return (mixed_share.astype(jnp.float32) + shared_share + routed).astype(jnp.bfloat16)


def solution(mesh):
    placed = (
        P("dp", None),
        P(),
        P(None, "head"),
        P(None, "head"),
        P(),
        P("head", None, None),
        P("head", None, None),
        P("head", None),
        P("dp", None, None),
        P("dp"),
        P("dp"),
        P(),
        P(),
        P("dp", None),
        P("dp", None, None, "head"),
        P("dp", "head", None),
        P(None, None, "head"),
        P("head", None),
    )
    return jax.shard_map(
        body, mesh=mesh, in_specs=placed, out_specs=P("dp", "head"), check_vma=False
    )
```

profile of v0, /device:TPU:1, one launch (start us, length us, event | category | flops | bytes accessed | tf_op | source)
XLA Modules:
  0.0 187.7 jit_solution(8351223471823655975)
XLA Ops:
  6.6 0.8 convert_element_type.107
  7.4 0.9 iota_compare_fusion.2
  8.2 1.0 fusion.40
  9.3 1.5 fusion.29
  10.8 10.4 %all-gather = bf16[4,144,32]{1,2,0:T(8,128)(2,1)S(1)} all-gather(bf16[1,144,32]{1,2,0:T(8,128)(2,1)S(1)} %fusion.29), channel_id=1, replica_groups=mesh['dp'=32,'head'=4] {'head'}, dimensions={0}, use_global_device_ids=true | all-gather | bytes 46080 | tf_op jit(solution)/shard_map/all_gather | solution.py:81
  21.5 1.6 fusion.61
  23.4 1.2 fusion.26
  25.3 3.4 %fusion.78 = (f32[32,4]{1,0:T(8,128)S(1)}, f32[32,4,128]{2,1,0:T(4,128)S(1)}) fusion(bf16[32,128,576]{1,2,0:T(8,128)(2,1)} %param.26, bf16[32,4,576]{2,0,1:T(8,128)(2,1)S(1)} %pad_maximum_fusion, pred[32,128]{1,0:T(8,128)(4,1)S(1)} %iota_compare_fusion.2), kind=kOutput, calls=%fused_computation.128 | convolution fusion | flops 18923392 | bytes 4936192 | tf_op jit(solution)/shard_map/rhc,rjc->rhj/dot_general | solution.py:88
  29.1 1.2 fusion.23
  30.8 1.1 convolution_convert_fusion.1
  33.8 41.9 %all-reduce.3.cloned.1.call-done = bf16[32,2048]{1,0:T(8,128)(2,1)} async-done(((bf16[32,2048]{1,0:T(8,128)(2,1)}), bf16[32,2048]{1,0:T(8,128)(2,1)}) %all-reduce.3.cloned.1.call-update) | async-done | bytes 131088 | tf_op jit(solution)/shard_map/psum | solution.py:116
  75.7 1.1 fusion.37
  77.5 5.6 %scatter_custom_fusion = bf16[384,2048]{1,0:T(8,128)(2,1)} fusion(s32[192]{0:T(256)S(1)} %bitcast.114, bf16[32,2048]{1,0:T(8,128)(2,1)S(1)} %fusion.39, s32[1024]{0:T(1024)S(1)} %pad_clamp_fusion.1, bf16[]{:T(256)} %constant.75.clone.1), kind=kCustom, calls=%fused_computation.28 | custom fusion | bytes 1572866 | tf_op jit(solution)/shard_map/scatter | solution.py:144
  83.1 3.7 %reshape.317 = bf16[32,2,6,2048]{3,2,1,0:T(8,128)(2,1)} reshape(bf16[384,2048]{1,0:T(8,128)(2,1)} %scatter_custom_fusion) | data formatting | bytes 3145728 | tf_op jit(solution)/shard_map/reshape | solution.py:147
  86.8 3.2 %copy.96 = bf16[32,2,6,2048]{3,1,2,0:T(2,128)(2,1)S(1)} copy(bf16[32,2,6,2048]{3,2,1,0:T(8,128)(2,1)} %reshape.317) | data formatting | bytes 3145728 | tf_op jit(solution)/shard_map/reshape | solution.py:147
  90.0 32.3 %all_to_all.10 = bf16[32,2,6,2048]{3,1,2,0:T(2,128)(2,1)S(1)} all-to-all(bf16[32,2,6,2048]{3,1,2,0:T(2,128)(2,1)S(1)} %copy.96), channel_id=1, replica_groups=mesh['dp'=32,'head'=4] {'dp'}, dimensions={0} | all-to-all | bytes 3145728 | tf_op jit(solution)/shard_map/all_to_all | solution.py:146
  122.4 5.9 %fusion.15 = f32[32,2,6,2,352]{4,0,3,2,1:T(8,128)S(1)} fusion(bf16[2,2048,2,352]{1,3,2,0:T(8,128)(2,1)} %param.32, bf16[32,2,6,2048,1]{3,1,2,0,4:T(2,128)(2,1)S(1)} %bitcast.106), kind=kOutput, calls=%fused_computation.17 | convolution fusion | flops 1107296256 | bytes 8421376 | tf_op jit(solution)/shard_map/secd,edkf->seckf/dot_general | solution.py:153
  128.3 2.2 %fusion.11 = bf16[32,2,6,2048]{3,0,2,1:T(8,128)(2,1)} fusion(bf16[2,352,2048]{2,1,0:T(8,128)(2,1)S(1)} %copy-done.10, f32[32,2,6,2,352]{4,0,3,2,1:T(8,128)S(1)} %fusion.15), kind=kOutput, calls=%fused_computation.13 | convolution fusion | flops 555245568 | bytes 5537792 | tf_op jit(solution)/shard_map/secf,efd->secd/dot_general | solution.py:157
  131.3 1.1 fusion.79
  132.4 1.6 gather_fusion.1
  134.3 2.9 %fusion.6 = f32[32,2,352]{2,0,1:T(8,128)S(1)} fusion(bf16[2048,2,352]{0,2,1:T(8,128)(2,1)} %param.34, bf16[32,2048]{1,0:T(8,128)(2,1)S(1)} %fusion.39), kind=kOutput, calls=%fused_computation.10 | convolution fusion | flops 92274688 | bytes 3104768 | tf_op jit(solution)/shard_map/dot_general | solution.py:174
  137.2 1.0 convolution_convert_fusion
  138.3 13.7 %reduce-scatter.5.cloned.1.call-done = bf16[32,2,6,512]{3,0,2,1:T(8,128)(2,1)} async-done(((bf16[32,2,6,2048]{3,0,2,1:T(8,128)(2,1)}), bf16[32,2,6,512]{3,0,2,1:T(8,128)(2,1)}) %reduce-scatter.5.cloned.1.call-update) | async-done | bytes 393232 | tf_op jit(solution)/shard_map/reduce_scatter | solution.py:160
  151.9 2.1 %copy.99 = bf16[32,2,6,512]{3,1,2,0:T(2,128)(2,1)} copy(bf16[32,2,6,512]{3,0,2,1:T(8,128)(2,1)} %reduce-scatter.5.cloned.1.call-done) | data formatting | bytes 786432 | tf_op jit(solution)/shard_map/reduce_scatter | solution.py:160
  154.1 8.6 %all-to-all-start.1 = ((bf16[32,2,6,512]{3,1,2,0:T(2,128)(2,1)}), bf16[32,2,6,512]{3,1,2,0:T(2,128)(2,1)S(1)}, u32[]{:S(2)}, u32[]{:S(2)}) async-start(bf16[32,2,6,512]{3,1,2,0:T(2,128)(2,1)} %copy.99), calls=%async_computation.3 | async-start | bytes 786432 | tf_op jit(solution)/shard_map/all_to_all | solution.py:163
  164.0 8.8 %all-to-all-done.1 = bf16[32,2,6,512]{3,1,2,0:T(2,128)(2,1)S(1)} async-done(((bf16[32,2,6,512]{3,1,2,0:T(2,128)(2,1)}), bf16[32,2,6,512]{3,1,2,0:T(2,128)(2,1)S(1)}, u32[]{:S(2)}, u32[]{:S(2)}) %all-to-all-start.1) | async-done | bytes 393248 | tf_op jit(solution)/shard_map/all_to_all | solution.py:163
  172.8 0.9 copy.100
  173.7 1.2 reshape.318
  174.9 1.8 gather_fusion
  176.7 1.8 reshape.320
  178.4 1.3 multiply_reduce_fusion
  179.7 1.4 add_convert_fusion
  (83 shorter events, 7.2 us)
Async XLA Ops:
  6.5 14.9 %copy-start = (bf16[2048,768]{1,0:T(8,128)(2,1)S(1)}, bf16[2048,768]{1,0:T(8,128)(2,1)}, u32[]{:S(2)}) copy-start(bf16[2048,768]{1,0:T(8,128)(2,1)} %param.20) | copy-start | bytes 9437188
  6.5 69.2 %all-reduce.3.cloned.1.call-start = ((), (), s32[]{:S(2)}) async-start(), calls=%async_computation.4 | async-start | bytes 262144 | tf_op jit(solution)/shard_map/psum | solution.py:116
  21.2 2.2 %copy-start.9 = (f32[512]{0:T(512)S(1)}, f32[512]{0:T(512)}, u32[]{:S(2)}) copy-start(f32[512]{0:T(512)} %param.22) | copy-start | bytes 6148
  25.3 3.8 %copy-start.1 = (bf16[32,128,576]{1,2,0:T(8,128)(2,1)S(1)}, bf16[32,128,576]{1,2,0:T(8,128)(2,1)}, u32[]{:S(2)}) copy-start(bf16[32,128,576]{1,2,0:T(8,128)(2,1)} %param.26) | copy-start | bytes 14155780
  29.1 1.2 copy-start.6
  29.1 1.8 copy-start.3
  30.3 1.7 copy-start.11
  30.3 2.1 %copy-start.7 = (s32[32,6]{0,1:T(8,128)S(1)}, s32[32,6]{0,1:T(8,128)}, u32[]{:S(2)}) copy-start(s32[32,6]{0,1:T(8,128)} %param.31) | copy-start | bytes 2308
  30.3 45.4 %copy-start.2 = (bf16[32,2048]{1,0:T(8,128)(2,1)S(1)}, bf16[32,2048]{1,0:T(8,128)(2,1)}, u32[]{:S(2)}) copy-start(bf16[32,2048]{1,0:T(8,128)(2,1)} %param.18) | copy-start | bytes 393220
  30.3 47.1 %copy-start.8 = (f32[2048]{0:T(1024)S(1)}, f32[2048]{0:T(1024)}, u32[]{:S(2)}) copy-start(f32[2048]{0:T(1024)} %param.29) | copy-start | bytes 24580
  32.0 120.0 %reduce-scatter.5.cloned.1.call-start = ((), (), s32[]{:S(2)}) async-start(), calls=%async_computation.6 | async-start | bytes 1966080 | tf_op jit(solution)/shard_map/reduce_scatter | solution.py:160
  76.8 0.6 copy-start.5
  122.4 5.9 %copy-start.10 = (bf16[2,352,2048]{2,1,0:T(8,128)(2,1)S(1)}, bf16[2,352,2048]{2,1,0:T(8,128)(2,1)}, u32[]{:S(2)}) copy-start(bf16[2,352,2048]{2,1,0:T(8,128)(2,1)} %param.33) | copy-start | bytes 8650756
  130.4 49.3 %reduce-scatter.3.cloned.1.call-start = ((), (), s32[]{:S(2)}) async-start(), calls=%async_computation.5 | async-start | bytes 163840 | tf_op jit(solution)/shard_map/reduce_scatter | solution.py:181
  134.3 3.0 %copy-start.4 = (bf16[352,2048]{1,0:T(8,128)(2,1)S(1)}, bf16[352,2048]{1,0:T(8,128)(2,1)}, u32[]{:S(2)}) copy-start(bf16[352,2048]{1,0:T(8,128)(2,1)} %param.35) | copy-start | bytes 4325380
  154.1 18.7 %all-to-all-start.1 = ((bf16[32,2,6,512]{3,1,2,0:T(2,128)(2,1)}), bf16[32,2,6,512]{3,1,2,0:T(2,128)(2,1)S(1)}, u32[]{:S(2)}, u32[]{:S(2)}) async-start(bf16[32,2,6,512]{3,1,2,0:T(2,128)(2,1)} %copy.99), calls=%async_computation.3 | async-start | bytes 786432 | tf_op jit(solution)/shard_map/all_to_all | solution.py:163
Sparse Core Ops, SparseCore 0:
  32.1 43.5 all-reduce.2
  130.6 21.3 reduce-scatter.4
  154.4 19.3 reduce-scatter.2
where the time goes:
time: 188 us
  waiting for transfers between devices  64.4 us (34%)
  blocking collectives  42.7 us (23%)
  local copies, waits for them, and re-layouts  25.4 us (14%)
  matrix products  23.6 us (13%)
  between operations  13.4 us (7%)
  other arithmetic  9.43 us (5%)
  starting transfers between devices  8.64 us (5%)
    psum x1, waiting for transfers between devices, body(): lax.psum(partial_value.astype(jnp.bfloat16), 'head').astype(jnp.float32)  41.9 us
    all_to_all x1, blocking collectives, body(): lax.all_to_all(packed.reshape(dp_count, local_experts, capacity, ffn_inpu...  32.3 us
    reduce_scatter x1, waiting for transfers between devices, body(): lax.psum_scatter(expert_part.astype(jnp.bfloat16), 'head', scatter_dimens...  13.7 us
    all_gather x1, blocking collectives, body(): fresh_kv = lax.all_gather(fresh_part, 'head', axis=1, tiled=True)  10.4 us
    all_to_all x1, waiting for transfers between devices, body(): lax.all_to_all(expert_share, 'dp', split_axis=0, concat_axis=0, tiled=True)  8.77 us
    all_to_all x1, starting transfers between devices, body(): lax.all_to_all(expert_share, 'dp', split_axis=0, concat_axis=0, tiled=True)  8.56 us
    reshape x2, local copies, waits for them, and re-layouts, body(): packed.reshape(dp_count, local_experts, capacity, ffn_input.shape[1])  6.93 us
    dot_general x1, matrix products, body(): jnp.einsum('secd,edkf->seckf', arrived, w_experts_in, preferred_element_t...  5.86 us
  transfers between devices with their start and end apart: 4, of which 3 were waited for; matrix products, arithmetic and copies ran while one was open for 11% of the time, Pallas kernels for 0%

commit v1 on v0

--- a/solution.py
+++ b/solution.py
@@ -11,6 +11,12 @@
 norm_eps = 1e-06
 rope_theta = 50000.0
 route_scale = 2.446
+
+
+def fill_the_roots(work_x):
+    view_out = jax.lax.all_gather(work_x, "head")
+    g_now = jnp.sum(view_out, 0)
+    return g_now
 
 
 def rms_norm(values, weights):
@@ -113,7 +119,7 @@
     partial_value = jnp.dot(
         values.reshape(request_count, local_heads * VDIM), w_out, preferred_element_type=jnp.float32
     )
-    attention = lax.psum(partial_value.astype(jnp.bfloat16), "head").astype(jnp.float32)
+    attention = fill_the_roots(partial_value.astype(jnp.bfloat16)).astype(jnp.float32)
     mixed_rows = (hidden.astype(jnp.float32) + attention).astype(jnp.bfloat16)
     ffn_input = rms_norm(mixed_rows.astype(jnp.float32), mlp_gain).astype(jnp.bfloat16)
     mixed_share = lax.dynamic_slice_in_dim(mixed_rows, column_start, share_width, 1)

time: 188 us -> 172 us (0.915)
  waiting for transfers between devices: 64.4 us -> 22 us
  blocking collectives: 42.7 us -> 58.3 us
  other arithmetic: 9.43 us -> 18.7 us
  local copies, waits for them, and re-layouts: 25.4 us -> 27.4 us
    psum x1 -> x0, waiting for transfers between devices: 41.9 us -> none  [body(): lax.psum(partial_value.astype(jnp.bfloat16), 'head').astype(jnp.float32)]
    all_gather x0 -> x1, blocking collectives: none -> 10.6 us  [fill_the_roots(): view_out = jax.lax.all_gather(work_x, 'head')]
    all_to_all x1, blocking collectives: 32.3 us -> 37.2 us  [body(): lax.all_to_all(packed.reshape(dp_count, local_experts, capacity, ffn_inpu...]
  transfers between devices with their start and end apart: 4 -> 3, of which waited for: 3 -> 2; matrix products, arithmetic and copies ran while one was open for 11% -> 11% of each run, Pallas kernels for 0% -> 0%
where the time goes in v1:
time: 172 us; the launch traced here: 171 us
  blocking collectives  58.3 us (34%)
  local copies, waits for them, and re-layouts  27.4 us (16%)
  matrix products  22.9 us (13%)
  waiting for transfers between devices  22 us (13%)
  other arithmetic  18.7 us (11%)
  between operations  13.7 us (8%)
  starting transfers between devices  8.49 us (5%)
    all_to_all x1, blocking collectives, body(): lax.all_to_all(packed.reshape(dp_count, local_experts, capacity, ffn_inpu...  37.2 us
    reduce_scatter x1, waiting for transfers between devices, body(): lax.psum_scatter(expert_part.astype(jnp.bfloat16), 'head', scatter_dimens...  14.4 us
    all_gather x1, blocking collectives, fill_the_roots(): view_out = jax.lax.all_gather(work_x, 'head')  10.6 us
    all_gather x1, blocking collectives, body(): fresh_kv = lax.all_gather(fresh_part, 'head', axis=1, tiled=True)  10.4 us
    all_to_all x1, starting transfers between devices, body(): lax.all_to_all(expert_share, 'dp', split_axis=0, concat_axis=0, tiled=True)  8.45 us
    all_to_all x1, waiting for transfers between devices, body(): lax.all_to_all(expert_share, 'dp', split_axis=0, concat_axis=0, tiled=True)  7.53 us
    reshape x2, local copies, waits for them, and re-layouts, body(): packed.reshape(dp_count, local_experts, capacity, ffn_input.shape[1])  6.93 us
    dot_general x1, matrix products, body(): jnp.einsum('secd,edkf->seckf', arrived, w_experts_in, preferred_element_t...  5.86 us
  transfers between devices with their start and end apart: 3, of which 2 were waited for; matrix products, arithmetic and copies ran while one was open for 11% of the time, Pallas kernels for 0%

profile of v1, /device:TPU:1, one launch (start us, length us, event | category | flops | bytes accessed | tf_op | source)
XLA Modules:
  0.0 171.4 jit_solution(15776220244076970243)
XLA Ops:
  9.8 1.2 convert_element_type.109
  13.2 1.0 fusion.40
  14.2 1.5 fusion.29
  15.7 10.4 %all-gather.1 = bf16[4,144,32]{1,2,0:T(8,128)(2,1)S(1)} all-gather(bf16[1,144,32]{1,2,0:T(8,128)(2,1)S(1)} %fusion.29), channel_id=1, replica_groups=mesh['dp'=32,'head'=4] {'head'}, dimensions={0}, use_global_device_ids=true | all-gather | bytes 46080 | tf_op jit(solution)/shard_map/all_gather | solution.py:87
  26.9 1.6 fusion.61
  28.8 1.3 pad_clamp_fusion.1
  34.7 1.2 fusion.26
  37.2 3.4 %fusion.78 = (f32[32,4]{1,0:T(8,128)S(1)}, f32[32,4,128]{2,1,0:T(4,128)S(1)}) fusion(bf16[32,128,576]{1,2,0:T(8,128)(2,1)} %param.26, bf16[32,4,576]{2,0,1:T(8,128)(2,1)S(1)} %pad_maximum_fusion, pred[32,128]{1,0:T(8,128)(4,1)S(1)} %iota_compare_fusion.2), kind=kOutput, calls=%fused_computation.128 | convolution fusion | flops 18923392 | bytes 4936192 | tf_op jit(solution)/shard_map/rhc,rjc->rhj/dot_general | solution.py:94
  40.9 1.2 fusion.23
  43.2 10.6 %all-gather = bf16[128,2048]{1,0:T(8,128)(2,1)} all-gather(bf16[32,2048]{1,0:T(8,128)(2,1)S(1)} %convolution_convert_fusion.1), channel_id=2, replica_groups=mesh['dp'=32,'head'=4] {'head'}, dimensions={0}, use_global_device_ids=true | all-gather | bytes 655360 | tf_op jit(solution)/shard_map/all_gather | solution.py:17
  53.8 1.1 reduce_sum.80
  55.9 5.7 %scatter_custom_fusion = bf16[384,2048]{1,0:T(8,128)(2,1)} fusion(s32[192]{0:T(256)S(1)} %bitcast.117, bf16[32,2048]{1,0:T(8,128)(2,1)S(1)} %fusion.39, s32[1024]{0:T(1024)} %pad_clamp_fusion.1, bf16[]{:T(256)} %constant.23.clone.1), kind=kCustom, calls=%fused_computation.28 | custom fusion | bytes 1573376 | tf_op jit(solution)/shard_map/scatter | solution.py:150
  61.6 3.7 %reshape.317 = bf16[32,2,6,2048]{3,2,1,0:T(8,128)(2,1)} reshape(bf16[384,2048]{1,0:T(8,128)(2,1)} %scatter_custom_fusion) | data formatting | bytes 3145728 | tf_op jit(solution)/shard_map/reshape | solution.py:153
  65.3 3.2 %copy.96 = bf16[32,2,6,2048]{3,1,2,0:T(2,128)(2,1)S(1)} copy(bf16[32,2,6,2048]{3,2,1,0:T(8,128)(2,1)} %reshape.317) | data formatting | bytes 3145728 | tf_op jit(solution)/shard_map/reshape | solution.py:153
  68.5 37.2 %all_to_all.10 = bf16[32,2,6,2048]{3,1,2,0:T(2,128)(2,1)S(1)} all-to-all(bf16[32,2,6,2048]{3,1,2,0:T(2,128)(2,1)S(1)} %copy.96), channel_id=1, replica_groups=mesh['dp'=32,'head'=4] {'dp'}, dimensions={0} | all-to-all | bytes 3145728 | tf_op jit(solution)/shard_map/all_to_all | solution.py:152
  105.8 5.9 %fusion.15 = f32[32,2,6,2,352]{4,0,3,2,1:T(8,128)S(1)} fusion(bf16[2,2048,2,352]{1,3,2,0:T(8,128)(2,1)} %param.32, bf16[32,2,6,2048,1]{3,1,2,0,4:T(2,128)(2,1)S(1)} %bitcast.108), kind=kOutput, calls=%fused_computation.17 | convolution fusion | flops 1107296256 | bytes 8421376 | tf_op jit(solution)/shard_map/secd,edkf->seckf/dot_general | solution.py:159
  111.6 2.2 %fusion.11 = bf16[32,2,6,2048]{3,0,2,1:T(8,128)(2,1)} fusion(bf16[2,352,2048]{2,1,0:T(8,128)(2,1)S(1)} %copy-done.11, f32[32,2,6,2,352]{4,0,3,2,1:T(8,128)S(1)} %fusion.15), kind=kOutput, calls=%fused_computation.13 | convolution fusion | flops 555245568 | bytes 5537792 | tf_op jit(solution)/shard_map/secf,efd->secd/dot_general | solution.py:163
  113.9 2.9 %fusion.6 = f32[32,2,352]{2,0,1:T(8,128)S(1)} fusion(bf16[2048,2,352]{0,2,1:T(8,128)(2,1)} %param.34, bf16[32,2048]{1,0:T(8,128)(2,1)S(1)} %fusion.39), kind=kOutput, calls=%fused_computation.10 | convolution fusion | flops 92274688 | bytes 3104768 | tf_op jit(solution)/shard_map/dot_general | solution.py:180
  116.8 1.0 convolution_convert_fusion
  118.1 1.1 fusion.79
  119.2 1.6 gather_fusion.1
  121.1 14.4 %reduce-scatter.5.cloned.1.call-done = bf16[32,2,6,512]{3,0,2,1:T(8,128)(2,1)} async-done(((bf16[32,2,6,2048]{3,0,2,1:T(8,128)(2,1)}), bf16[32,2,6,512]{3,0,2,1:T(8,128)(2,1)}) %reduce-scatter.5.cloned.1.call-update) | async-done | bytes 393232 | tf_op jit(solution)/shard_map/reduce_scatter | solution.py:166
  135.4 2.1 %copy.99 = bf16[32,2,6,512]{3,1,2,0:T(2,128)(2,1)} copy(bf16[32,2,6,512]{3,0,2,1:T(8,128)(2,1)} %reduce-scatter.5.cloned.1.call-done) | data formatting | bytes 786432 | tf_op jit(solution)/shard_map/reduce_scatter | solution.py:166
  137.6 8.4 %all-to-all-start.1 = ((bf16[32,2,6,512]{3,1,2,0:T(2,128)(2,1)}), bf16[32,2,6,512]{3,1,2,0:T(2,128)(2,1)S(1)}, u32[]{:S(2)}, u32[]{:S(2)}) async-start(bf16[32,2,6,512]{3,1,2,0:T(2,128)(2,1)} %copy.99), calls=%async_computation.3 | async-start | bytes 786432 | tf_op jit(solution)/shard_map/all_to_all | solution.py:169
  147.4 1.3 pad_clamp_fusion
  148.7 7.5 %all-to-all-done.1 = bf16[32,2,6,512]{3,1,2,0:T(2,128)(2,1)S(1)} async-done(((bf16[32,2,6,512]{3,1,2,0:T(2,128)(2,1)}), bf16[32,2,6,512]{3,1,2,0:T(2,128)(2,1)S(1)}, u32[]{:S(2)}, u32[]{:S(2)}) %all-to-all-start.1) | async-done | bytes 393248 | tf_op jit(solution)/shard_map/all_to_all | solution.py:169
  156.2 0.9 copy.100
  157.1 1.2 reshape.318
  158.3 1.8 %gather_fusion = bf16[192,512]{1,0:T(8,128)(2,1)} fusion(bf16[384,512]{1,0:T(8,128)(2,1)S(1)} %reshape.318, s32[1024]{0:T(1024)} %pad_clamp_fusion), kind=kCustom, calls=%fused_computation.1 | custom fusion | bytes 393984 | tf_op jit(solution)/shard_map/gather | solution.py:172
  160.1 1.8 %reshape.320 = f32[32,6,512]{2,1,0:T(8,128)} reshape(bf16[192,512]{1,0:T(8,128)(2,1)} %gather_fusion) | data formatting | bytes 589824 | tf_op jit(solution)/shard_map/convert_element_type | solution.py:172
  161.8 1.3 multiply_reduce_fusion
  163.1 1.4 add_convert_fusion
  (84 shorter events, 16.5 us)
Async XLA Ops:
  6.5 20.4 %copy-start = (bf16[2048,768]{1,0:T(8,128)(2,1)S(1)}, bf16[2048,768]{1,0:T(8,128)(2,1)}, u32[]{:S(2)}) copy-start(bf16[2048,768]{1,0:T(8,128)(2,1)} %param.20) | copy-start | bytes 9437188
  6.5 128.9 %reduce-scatter.5.cloned.1.call-start = ((), (), s32[]{:S(2)}) async-start(), calls=%async_computation.5 | async-start | bytes 1966080 | tf_op jit(solution)/shard_map/reduce_scatter | solution.py:166
  37.2 3.8 %copy-start.1 = (bf16[32,128,576]{1,2,0:T(8,128)(2,1)S(1)}, bf16[32,128,576]{1,2,0:T(8,128)(2,1)}, u32[]{:S(2)}) copy-start(bf16[32,128,576]{1,2,0:T(8,128)(2,1)} %param.26) | copy-start | bytes 14155780
  40.9 1.2 copy-start.6
  40.9 1.8 %copy-start.3 = (bf16[512,2048]{1,0:T(8,128)(2,1)S(1)}, bf16[512,2048]{1,0:T(8,128)(2,1)}, u32[]{:S(2)}) copy-start(bf16[512,2048]{1,0:T(8,128)(2,1)} %param.25) | copy-start | bytes 6291460
  42.2 12.8 %copy-start.2 = (bf16[32,2048]{1,0:T(8,128)(2,1)S(1)}, bf16[32,2048]{1,0:T(8,128)(2,1)}, u32[]{:S(2)}) copy-start(bf16[32,2048]{1,0:T(8,128)(2,1)} %param.18) | copy-start | bytes 393220
  42.7 12.4 %copy-start.9 = (pred[192,1]{0,1:T(4,128)(4,1)S(1)}, pred[192,1]{0,1:T(4,128)(4,1)}, u32[]{:S(2)}) copy-start(pred[192,1]{0,1:T(4,128)(4,1)} %eq.57) | copy-start | bytes 580
  42.7 12.4 %copy-start.10 = (s32[192,1]{0,1:T(1,128)S(1)}, s32[192,1]{0,1:T(1,128)}, u32[]{:S(2)}) copy-start(s32[192,1]{0,1:T(1,128)} %mul.265) | copy-start | bytes 2308
  42.7 13.0 %copy-start.8 = (f32[2048]{0:T(1024)S(1)}, f32[2048]{0:T(1024)}, u32[]{:S(2)}) copy-start(f32[2048]{0:T(1024)} %param.29) | copy-start | bytes 24580
  55.1 0.6 copy-start.5
  105.8 5.9 %copy-start.11 = (bf16[2,352,2048]{2,1,0:T(8,128)(2,1)S(1)}, bf16[2,352,2048]{2,1,0:T(8,128)(2,1)}, u32[]{:S(2)}) copy-start(bf16[2,352,2048]{2,1,0:T(8,128)(2,1)} %param.33) | copy-start | bytes 8650756
  113.8 4.0 %copy-start.7 = (s32[32,6]{0,1:T(8,128)S(1)}, s32[32,6]{0,1:T(8,128)}, u32[]{:S(2)}) copy-start(s32[32,6]{0,1:T(8,128)} %param.31) | copy-start | bytes 2308
  113.8 49.3 %reduce-scatter.3.cloned.1.call-start = ((), (), s32[]{:S(2)}) async-start(), calls=%async_computation.4 | async-start | bytes 163840 | tf_op jit(solution)/shard_map/reduce_scatter | solution.py:187
  113.9 2.9 %copy-start.4 = (bf16[352,2048]{1,0:T(8,128)(2,1)S(1)}, bf16[352,2048]{1,0:T(8,128)(2,1)}, u32[]{:S(2)}) copy-start(bf16[352,2048]{1,0:T(8,128)(2,1)} %param.35) | copy-start | bytes 4325380
  119.2 26.8 %copy-start.12 = (s32[32]{0:T(128)S(1)}, s32[32]{0:T(128)}, u32[]{:S(2)}) copy-start(s32[32]{0:T(128)} %param.28) | copy-start | bytes 388
  137.6 18.6 %all-to-all-start.1 = ((bf16[32,2,6,512]{3,1,2,0:T(2,128)(2,1)}), bf16[32,2,6,512]{3,1,2,0:T(2,128)(2,1)S(1)}, u32[]{:S(2)}, u32[]{:S(2)}) async-start(bf16[32,2,6,512]{3,1,2,0:T(2,128)(2,1)} %copy.99), calls=%async_computation.3 | async-start | bytes 786432 | tf_op jit(solution)/shard_map/all_to_all | solution.py:169
Sparse Core Ops, SparseCore 0:
  114.0 21.4 reduce-scatter.4
  137.8 19.2 reduce-scatter.2
